TPU v7x, 512 devices: a whole 4x4x16 slice. The times are simulated.
512 devices in a mesh: dp: 64 (over z, x_lo, core), lon: 8 (over y, x_hi).
Axes of the slice: x: 4 (x_hi: 2, x_lo: 2; x = x_hi * 2 + x_lo), y: 4, z: 16, core: 2. Of those that a mesh axis runs over, the one named last changes fastest.
Arguments:
- features: bfloat16 [64, 72, 48, 1152], P('dp', 'lon'), may hold values from -6 to 6
- depth_w: bfloat16 [2, 3, 3, 1152], replicated, may hold values from -2 to 2
- point_w: bfloat16 [2, 1152, 256], replicated, may hold values from -0.1875 to 0.1875
- point_bias: float32 [2, 256], replicated, may hold values from -3 to 3
- cotangent: bfloat16 [64, 72, 48, 512], P('dp', 'lon'), may hold values from -6 to 6
Outputs:
- feature_grad: bfloat16 [64, 72, 48, 1152], P('dp', 'lon')
- depth_grad: bfloat16 [2, 3, 3, 1152], replicated
- point_grad: bfloat16 [2, 1152, 256], replicated
- bias_grad: float32 [2, 256], replicated
All inputs are finite; a program needn't handle non-finite values.
Results may differ from a plain program's by a relative error of at most 0.0075.
Values may be sent and summed in bfloat16 or wider, within the bound.
No kernel may reach another device: no remote copies, remote signals or barrier semaphores. Data moves between devices by JAX's collectives and lax.ppermute only.
A program may use at most 128 MiB of HBM per device.

v0:
```python
import jax
import jax.numpy as jnp
from jax import lax
from jax.sharding import PartitionSpec as P

RATE_A = 24
RATE_B = 36


def from_behind(block, axis, distance):
    devices = range(lax.axis_size(axis))
    route = [((i - distance) % len(devices), i) for i in devices]
    return lax.ppermute(block, axis, route)


def lat_shift(grid_field, offset, axis_pos):
    height = grid_field.shape[axis_pos]
    if offset == 0:
        return grid_field
    widths = [(0, 0)] * grid_field.ndim
    if offset > 0:
        kept_rows = lax.slice_in_dim(grid_field, offset, height, axis=axis_pos)
        widths[axis_pos] = (0, offset)
    else:
        kept_rows = lax.slice_in_dim(grid_field, 0, height + offset, axis=axis_pos)
        widths[axis_pos] = (-offset, 0)
    return jnp.pad(kept_rows, widths)


def gate_slope(pre_act):
    sigmoid_val = jax.nn.sigmoid(pre_act)
    return sigmoid_val * (1.0 + pre_act * (1.0 - sigmoid_val))


def column_plan(dilation, direction, columns, group_size):
    run_list = []
    for column in range(columns):
        target = column + direction * dilation
        offset = target // columns
        local_col = target % columns
        if run_list and run_list[-1][0] == offset:
            run_list[-1][2] = local_col + 1
        else:
            run_list.append([offset, local_col, local_col + 1])
    return [(-entry[0] % group_size, entry[1], entry[2]) for entry in run_list]


def join_pieces(piece_list):
    if len(piece_list) == 1:
        return piece_list[0]
    return jnp.concatenate(piece_list, axis=1)


def fetch_each(grid_field, offset_pairs, group_size, send_fn):
    result = {}
    for offset_pair in offset_pairs:
        piece_list = []
        for shift_by, first_col, finish in column_plan(
            offset_pair[0], offset_pair[1], grid_field.shape[1], group_size
        ):
            column_piece = grid_field[:, first_col:finish]
            column_piece = send_fn(column_piece, shift_by)
            piece_list.append(column_piece)
        result[offset_pair] = join_pieces(piece_list)
    return result


def send_features(column_piece, shift_by):
    return from_behind(column_piece, "lon", shift_by)


def send_grads(column_piece, shift_by):
    return from_behind(column_piece, "lon", shift_by)


def per_device(features, depth_w, point_w, point_bias, cotangent):
    group_size = lax.axis_size("lon")
    channels = features.shape[3]
    outputs = point_w.shape[2]
    dilations = (RATE_A, RATE_B)
    offset_pairs = [(dilation, direction) for dilation in dilations for direction in (-1, 1)]
    moved_in = fetch_each(features, offset_pairs, group_size, send_features)
    depth_outs = []
    for branch, dilation in enumerate(dilations):
        depth_acc = jnp.zeros(features.shape, jnp.float32)
        for lon_step in (-1, 0, 1):
            source = features if lon_step == 0 else moved_in[dilation, lon_step]
            for lat_step in (-1, 0, 1):
                tapped = lat_shift(source, lat_step * dilation, 2).astype(jnp.float32)
                depth_acc = (
                    depth_acc
                    + depth_w[branch, lat_step + 1, lon_step + 1].astype(jnp.float32) * tapped
                )
        depth_outs.append(depth_acc.astype(jnp.bfloat16))
    point_terms = []
    bias_terms = []
    dgrad_list = []
    for branch, dilation in enumerate(dilations):
        flat_depth = depth_outs[branch].reshape(-1, channels)
        point_act = (
            jnp.dot(flat_depth, point_w[branch], preferred_element_type=jnp.float32)
            + point_bias[branch]
        )
        upstream_part = (
            cotangent[..., branch * outputs : (branch + 1) * outputs]
            .reshape(-1, outputs)
            .astype(jnp.float32)
        )
        pgrad = (upstream_part * gate_slope(point_act)).astype(jnp.bfloat16)
        bias_terms.append(jnp.sum(pgrad.astype(jnp.float32), axis=0))
        point_terms.append(
            lax.dot_general(
                flat_depth, pgrad, (((0,), (0,)), ((), ())), preferred_element_type=jnp.float32
            )
        )
        dgrad = lax.dot_general(
            pgrad, point_w[branch], (((1,), (1,)), ((), ())), preferred_element_type=jnp.float32
        )
        dgrad_list.append(dgrad.astype(jnp.bfloat16).reshape(features.shape))
    point_local = jnp.stack(point_terms)
    bias_local = jnp.stack(bias_terms)
    grad_field = jnp.zeros(features.shape, jnp.float32)
    depth_terms = []
    for branch, dilation in enumerate(dilations):
        branch_pairs = [(dilation, -1), (dilation, 1)]
        moved_back = fetch_each(dgrad_list[branch], branch_pairs, group_size, send_grads)
        dgrad_wide = dgrad_list[branch].astype(jnp.float32)
        tap_rows = []
        for lat_step in (-1, 0, 1):
            tap_cols = []
            for lon_step in (-1, 0, 1):
                source = features if lon_step == 0 else moved_in[dilation, lon_step]
                tapped = lat_shift(source, lat_step * dilation, 2).astype(jnp.float32)
                tap_cols.append(jnp.sum(tapped * dgrad_wide, axis=(0, 1, 2)))
                behind = dgrad_list[branch] if lon_step == 0 else moved_back[dilation, -lon_step]
                behind = lat_shift(behind, -lat_step * dilation, 2).astype(jnp.float32)
                grad_field = (
                    grad_field
                    + depth_w[branch, lat_step + 1, lon_step + 1].astype(jnp.float32) * behind
                )
            tap_rows.append(jnp.stack(tap_cols))
        depth_terms.append(jnp.stack(tap_rows))
    depth_local = jnp.stack(depth_terms)
    feature_grad = grad_field.astype(jnp.bfloat16)
    point_sum, depth_sum, bias_sum = lax.psum((point_local, depth_local, bias_local), ("dp", "lon"))
    images = lax.axis_size("dp") * features.shape[0]
    depth_grad = (depth_sum / images).astype(jnp.bfloat16)
    point_grad = (point_sum / images).astype(jnp.bfloat16)
    bias_grad = bias_sum / images
    return (feature_grad, depth_grad, point_grad, bias_grad)


def solution(mesh):
    placed = (P("dp", "lon", None, None), P(), P(), P(), P("dp", "lon", None, None))
    return jax.shard_map(
        per_device,
        mesh=mesh,
        in_specs=placed,
        out_specs=(P("dp", "lon", None, None), P(), P(), P()),
        check_vma=False,
    )
```

profile of v0, /device:TPU:1, one launch (start us, length us, event | category | flops | bytes accessed | tf_op | source)
XLA Modules:
  0.0 733.2 jit_solution(12406998658973591604)
XLA Ops:
  7.2 5.8 collective-permute-start.8
  13.0 1.4 fusion.71
  14.4 4.8 collective-permute-start
  19.3 2.1 collective-permute-start.1
  21.3 5.4 collective-permute-start.3
  26.8 3.0 collective-permute-start.2
  30.3 42.3 %collective-permute-done.2 = bf16[1,3,48,1152]{3,2,1,0:T(8,128)(2,1)S(1)} collective-permute-done((bf16[1,3,48,1152]{3,2,1,0:T(8,128)(2,1)S(1)}, bf16[1,3,48,1152]{3,2,1,0:T(8,128)(2,1)S(1)}, u32[]{:S(2)}, u32[]{:S(2)}) %collective-permute-start.2) | collective-permute-done | bytes 331808 | tf_op jit(solution)/shard_map/ppermute | solution.py:13
  73.1 1.5 fusion.8
  75.2 0.7 fusion.26
  75.9 1.2 fusion.67
  77.0 0.8 fusion.68
  77.9 3.3 collective-permute-start.4
  81.2 0.9 fusion.63
  83.3 4.4 collective-permute-start.5
  87.7 3.3 collective-permute-start.6
  91.0 2.0 collective-permute-start.7
  93.0 1.5 convolution_bitcast_fusion.1
  94.5 0.8 constant_dynamic-update-slice_fusion.5
  95.4 1.4 fusion.15
  97.3 1.6 convolution_bitcast_fusion
  99.3 4.3 collective-permute-start.9
  103.6 2.3 fusion.41
  106.1 139.6 %psum.23 = f32[2,256]{1,0:T(2,128)S(1)} all-reduce(f32[2,256]{1,0:T(2,128)S(1)} %pad_maximum_fusion.2), channel_id=1, replica_groups=mesh['dp'=64,'lon'=8] {'dp','lon'}, use_global_device_ids=true, to_apply=%region_19.20 | all-reduce | flops 512 | bytes 4096 | tf_op jit(solution)/shard_map/psum | solution.py:145
  245.7 3.2 pad_maximum_fusion
  249.1 0.7 pad_maximum_fusion.1
  250.5 1.1 constant_dynamic-update-slice_fusion.7
  251.6 1.2 constant_dynamic-update-slice_fusion.4
  252.8 1.0 constant_dynamic-update-slice_fusion.6
  254.1 1.2 fusion.65
  255.5 5.0 fusion.25
  260.5 462.3 %all-reduce.23.cloned.1.call-done = (f32[2,3,3,1152]{3,2,1,0:T(4,128)}, f32[2,1152,256]{2,1,0:T(8,128)}) async-done(((f32[2,3,3,1152]{3,2,1,0:T(4,128)}, f32[2,1152,256]{2,1,0:T(8,128)}), (f32[2,3,3,1152]{3,2,1,0:T(4,128)}, f32[2,1152,256]{2,1,0:T(8,128)})) %all-reduce.23.cloned.1.call-update) | async-done | bytes 2442256 | tf_op jit(solution)/shard_map/psum | solution.py:145
  722.7 2.9 multiply_convert_fusion
  (115 shorter events, 5.6 us)
Async XLA Ops:
  7.2 12.0 %copy-start = (bf16[1,9,48,1152]{3,2,1,0:T(8,128)(2,1)S(1)}, bf16[1,9,48,1152]{3,2,1,0:T(8,128)(2,1)}, u32[]{:S(2)}) copy-start(bf16[1,9,48,1152]{3,2,1,0:T(8,128)(2,1)} %param.5) | copy-start | bytes 2985988
  7.2 715.6 %all-reduce.23.cloned.1.call-start = ((), (), s32[]{:S(2)}) async-start(), calls=%async_computation | async-start | bytes 4939776 | tf_op jit(solution)/shard_map/psum | solution.py:145
  7.2 88.0 %collective-permute-start.8 = (bf16[1,9,48,1152]{3,2,1,0:T(8,128)(2,1)}, bf16[1,9,48,1152]{3,2,1,0:T(8,128)(2,1)S(1)}, u32[]{:S(2)}, u32[]{:S(2)}) collective-permute-start(bf16[1,9,48,1152]{3,2,1,0:T(8,128)(2,1)} %param.5), channel_id=1, source_target_pairs={{4,0},{5,1},{6,2},{7,3},{0,4},{1,5},{2,6},{3,7},{12,8},{13,9},{14,... | collective-permute-start | bytes 2985992 | tf_op jit(solution)/shard_map/ppermute | solution.py:13
  14.4 58.2 %collective-permute-start = (bf16[1,6,48,1152]{3,2,1,0:T(8,128)(2,1)S(1)}, bf16[1,6,48,1152]{3,2,1,0:T(8,128)(2,1)S(1)}, u32[]{:S(2)}, u32[]{:S(2)}) collective-permute-start(bf16[1,6,48,1152]{3,2,1,0:T(8,128)(2,1)S(1)} %get-tuple-element.61), channel_id=1, source_target_pairs={{5,0},{6,1},{7,2},{0,3},{1,4},{2,5},{3,6},{4,7},{13,8},{14,9},{15,... | collective-permute-start | bytes 1990664 | tf_op jit(solution)/shard_map/ppermute | solution.py:13
  19.3 10.7 %copy-start.29 = (f32[2,256]{1,0:T(2,128)S(1)}, f32[2,256]{1,0:T(2,128)}, u32[]{:S(2)}) copy-start(f32[2,256]{1,0:T(2,128)} %param.8) | copy-start | bytes 6148
  19.3 10.7 %copy-start.5 = (bf16[2,3,3,1152]{3,0,2,1:T(2,128)(2,1)S(1)}, bf16[2,3,3,1152]{3,0,2,1:T(2,128)(2,1)}, u32[]{:S(2)}) copy-start(bf16[2,3,3,1152]{3,0,2,1:T(2,128)(2,1)} %param.6) | copy-start | bytes 124420
  19.3 10.9 %copy-start.3 = (bf16[1,9,48,512]{3,2,1,0:T(8,128)(2,1)S(1)}, bf16[1,9,48,512]{3,2,1,0:T(8,128)(2,1)}, u32[]{:S(2)}) copy-start(bf16[1,9,48,512]{3,2,1,0:T(8,128)(2,1)} %param.9) | copy-start | bytes 1327108
  19.3 53.4 %collective-permute-start.1 = (bf16[1,3,48,1152]{3,2,1,0:T(8,128)(2,1)S(1)}, bf16[1,3,48,1152]{3,2,1,0:T(8,128)(2,1)S(1)}, u32[]{:S(2)}, u32[]{:S(2)}) collective-permute-start(bf16[1,3,48,1152]{3,2,1,0:T(8,128)(2,1)S(1)} %get-tuple-element.59), channel_id=1, source_target_pairs={{6,0},{7,1},{0,2},{1,3},{2,4},{3,5},{4,6},{5,7},{14,8},{15,9},{8,1... | collective-permute-start | bytes 995336 | tf_op jit(solution)/shard_map/ppermute | solution.py:13
  21.3 51.5 %collective-permute-start.3 = (bf16[1,6,48,1152]{3,2,1,0:T(8,128)(2,1)S(1)}, bf16[1,6,48,1152]{3,2,1,0:T(8,128)(2,1)S(1)}, u32[]{:S(2)}, u32[]{:S(2)}) collective-permute-start(bf16[1,6,48,1152]{3,2,1,0:T(8,128)(2,1)S(1)} %get-tuple-element.62), channel_id=1, source_target_pairs={{3,0},{4,1},{5,2},{6,3},{7,4},{0,5},{1,6},{2,7},{11,8},{12,9},{13,... | collective-permute-start | bytes 1990664 | tf_op jit(solution)/shard_map/ppermute | solution.py:13
  26.8 45.8 %collective-permute-start.2 = (bf16[1,3,48,1152]{3,2,1,0:T(8,128)(2,1)S(1)}, bf16[1,3,48,1152]{3,2,1,0:T(8,128)(2,1)S(1)}, u32[]{:S(2)}, u32[]{:S(2)}) collective-permute-start(bf16[1,3,48,1152]{3,2,1,0:T(8,128)(2,1)S(1)} %get-tuple-element.60), channel_id=1, source_target_pairs={{2,0},{3,1},{4,2},{5,3},{6,4},{7,5},{0,6},{1,7},{10,8},{11,9},{12,... | collective-permute-start | bytes 995336 | tf_op jit(solution)/shard_map/ppermute | solution.py:13
  30.2 42.8 %copy-start.9 = (f32[1152]{0:T(1024)}, f32[1152]{0:T(1024)S(1)}, u32[]{:S(2)}) copy-start(f32[1152]{0:T(1024)S(1)} %get-tuple-element.23) | copy-start | bytes 13828
  30.2 42.8 %copy-start.11 = (f32[1152]{0:T(1024)}, f32[1152]{0:T(1024)S(1)}, u32[]{:S(2)}) copy-start(f32[1152]{0:T(1024)S(1)} %get-tuple-element.31) | copy-start | bytes 13828
  30.2 42.8 %copy-start.13 = (f32[1152]{0:T(1024)}, f32[1152]{0:T(1024)S(1)}, u32[]{:S(2)}) copy-start(f32[1152]{0:T(1024)S(1)} %get-tuple-element.32) | copy-start | bytes 13828
  30.2 42.8 %copy-start.15 = (f32[1152]{0:T(1024)}, f32[1152]{0:T(1024)S(1)}, u32[]{:S(2)}) copy-start(f32[1152]{0:T(1024)S(1)} %get-tuple-element.33) | copy-start | bytes 13828
  30.2 42.8 %copy-start.17 = (f32[1152]{0:T(1024)}, f32[1152]{0:T(1024)S(1)}, u32[]{:S(2)}) copy-start(f32[1152]{0:T(1024)S(1)} %get-tuple-element.34) | copy-start | bytes 13828
  30.3 42.8 %copy-start.19 = (f32[1152]{0:T(1024)}, f32[1152]{0:T(1024)S(1)}, u32[]{:S(2)}) copy-start(f32[1152]{0:T(1024)S(1)} %get-tuple-element.35) | copy-start | bytes 13828
  30.3 42.8 %copy-start.21 = (f32[1152]{0:T(1024)}, f32[1152]{0:T(1024)S(1)}, u32[]{:S(2)}) copy-start(f32[1152]{0:T(1024)S(1)} %get-tuple-element.36) | copy-start | bytes 13828
  30.3 42.8 %copy-start.23 = (f32[1152]{0:T(1024)}, f32[1152]{0:T(1024)S(1)}, u32[]{:S(2)}) copy-start(f32[1152]{0:T(1024)S(1)} %get-tuple-element.37) | copy-start | bytes 13828
  30.3 42.8 %copy-start.25 = (f32[1152]{0:T(1024)}, f32[1152]{0:T(1024)S(1)}, u32[]{:S(2)}) copy-start(f32[1152]{0:T(1024)S(1)} %get-tuple-element.38) | copy-start | bytes 13828
  30.3 65.1 %copy-start.7 = (f32[1152]{0:T(1024)}, f32[1152]{0:T(1024)S(1)}, u32[]{:S(2)}) copy-start(f32[1152]{0:T(1024)S(1)} %get-tuple-element.40) | copy-start | bytes 13828
  73.1 1.5 copy-start.4
  77.9 16.6 %collective-permute-start.4 = (bf16[1,3,48,1152]{3,2,1,0:T(8,128)(2,1)S(1)}, bf16[1,3,48,1152]{3,2,1,0:T(8,128)(2,1)S(1)}, u32[]{:S(2)}, u32[]{:S(2)}) collective-permute-start(bf16[1,3,48,1152]{3,2,1,0:T(8,128)(2,1)S(1)} %get-tuple-element.55), channel_id=1, source_target_pairs={{2,0},{3,1},{4,2},{5,3},{6,4},{7,5},{0,6},{1,7},{10,8},{11,9},{12,... | collective-permute-start | bytes 995336 | tf_op jit(solution)/shard_map/ppermute | solution.py:13
  83.3 168.3 %collective-permute-start.5 = (bf16[1,6,48,1152]{3,2,1,0:T(8,128)(2,1)}, bf16[1,6,48,1152]{3,2,1,0:T(8,128)(2,1)}, u32[]{:S(2)}, u32[]{:S(2)}) collective-permute-start(bf16[1,6,48,1152]{3,2,1,0:T(8,128)(2,1)} %get-tuple-element.53), channel_id=1, source_target_pairs={{3,0},{4,1},{5,2},{6,3},{7,4},{0,5},{1,6},{2,7},{11,8},{12,9},{13,... | collective-permute-start | bytes 1990664 | tf_op jit(solution)/shard_map/ppermute | solution.py:13
  87.7 162.7 %collective-permute-start.6 = (bf16[1,6,48,1152]{3,2,1,0:T(8,128)(2,1)}, bf16[1,6,48,1152]{3,2,1,0:T(8,128)(2,1)}, u32[]{:S(2)}, u32[]{:S(2)}) collective-permute-start(bf16[1,6,48,1152]{3,2,1,0:T(8,128)(2,1)} %get-tuple-element.54), channel_id=1, source_target_pairs={{5,0},{6,1},{7,2},{0,3},{1,4},{2,5},{3,6},{4,7},{13,8},{14,9},{15,... | collective-permute-start | bytes 1990664 | tf_op jit(solution)/shard_map/ppermute | solution.py:13
  91.0 161.8 %collective-permute-start.7 = (bf16[1,3,48,1152]{3,2,1,0:T(8,128)(2,1)}, bf16[1,3,48,1152]{3,2,1,0:T(8,128)(2,1)}, u32[]{:S(2)}, u32[]{:S(2)}) collective-permute-start(bf16[1,3,48,1152]{3,2,1,0:T(8,128)(2,1)} %get-tuple-element.56), channel_id=1, source_target_pairs={{6,0},{7,1},{0,2},{1,3},{2,4},{3,5},{4,6},{5,7},{14,8},{15,9},{8,1... | collective-permute-start | bytes 995336 | tf_op jit(solution)/shard_map/ppermute | solution.py:13
  99.3 154.8 %collective-permute-start.9 = (bf16[1,9,48,1152]{3,2,1,0:T(8,128)(2,1)S(1)}, bf16[1,9,48,1152]{3,2,1,0:T(8,128)(2,1)}, u32[]{:S(2)}, u32[]{:S(2)}) collective-permute-start(bf16[1,9,48,1152]{3,2,1,0:T(8,128)(2,1)S(1)} %bitcast.69), channel_id=1, source_target_pairs={{4,0},{5,1},{6,2},{7,3},{0,4},{1,5},{2,6},{3,7},{12,8},{13,9},{14,... | collective-permute-start | bytes 2985992 | tf_op jit(solution)/shard_map/ppermute | solution.py:13
  245.7 3.3 copy-start.27
  245.7 3.3 copy-start.28
  249.8 1.9 copy-start.1
  253.9 1.4 copy-start.2
  253.9 1.4 copy-start.8
  722.7 2.9 copy-start.6
  (9 other events, 12.9 us)
Sparse Core Ops, SparseCore 0:
  249.9 472.7 all-reduce.22
where the time goes:
time: 734 us; the launch traced here: 733 us
  waiting for transfers between devices  505 us (69%)
  blocking collectives  140 us (19%)
  starting transfers between devices  38.2 us (5%)
  other arithmetic  17.9 us (2%)
  between operations  14.9 us (2%)
  local copies, waits for them, and re-layouts  12.6 us (2%)
    psum x1, waiting for transfers between devices, per_device(): lax.psum((point_local, depth_local, bias_local), ('dp', 'lon'))  462 us
    psum x1, blocking collectives, per_device(): lax.psum((point_local, depth_local, bias_local), ('dp', 'lon'))  140 us
    ppermute x10, waiting for transfers between devices, from_behind(): return lax.ppermute(block, axis, route)  42.3 us
    ppermute x10, starting transfers between devices, from_behind(): return lax.ppermute(block, axis, route)  38.2 us
  transfers between devices with their start and end apart: 11, of which 2 were waited for; matrix products, arithmetic and copies ran while one was open for 4% of the time, Pallas kernels for 0%

commit v1 on v0

--- a/solution.py
+++ b/solution.py
@@ -142,7 +142,9 @@
         depth_terms.append(jnp.stack(tap_rows))
     depth_local = jnp.stack(depth_terms)
     feature_grad = grad_field.astype(jnp.bfloat16)
-    point_sum, depth_sum, bias_sum = lax.psum((point_local, depth_local, bias_local), ("dp", "lon"))
+    point_sum, depth_sum, bias_sum = lax.psum(
+        lax.psum((point_local, depth_local, bias_local), "dp"), "lon"
+    )
     images = lax.axis_size("dp") * features.shape[0]
     depth_grad = (depth_sum / images).astype(jnp.bfloat16)
     point_grad = (point_sum / images).astype(jnp.bfloat16)

time: 734 us -> 701 us (0.955)
  waiting for transfers between devices: 505 us -> 484 us
  blocking collectives: 140 us -> 129 us
    psum x1 -> x2, waiting for transfers between devices: 462 us -> 423 us  [the longest x1 291 us: per_device(): lax.psum((point_local, depth_local, bias_local), 'dp')]
    ppermute x10, waiting for transfers between devices: 42.3 us -> 61.1 us  [from_behind(): return lax.ppermute(block, axis, route)]
    psum x1 -> x2, blocking collectives: 140 us -> 129 us  [the longest x1 112 us: per_device(): lax.psum((point_local, depth_local, bias_local), 'dp')]
  transfers between devices with their start and end apart: 11 -> 12, of which waited for: 2 -> 4; matrix products, arithmetic and copies ran while one was open for 4% -> 4% of each run, Pallas kernels for 0% -> 0%
where the time goes in v1:
time: 701 us; the launch traced here: 700 us
  waiting for transfers between devices  484 us (69%)
  blocking collectives  129 us (18%)
  starting transfers between devices  36.7 us (5%)
  other arithmetic  16.9 us (2%)
  between operations  15 us (2%)
  local copies, waits for them, and re-layouts  13.9 us (2%)
    psum x1, waiting for transfers between devices, per_device(): lax.psum((point_local, depth_local, bias_local), 'dp')  291 us
    psum x1, waiting for transfers between devices, per_device(): lax.psum(lax.psum((point_local, depth_local, bias_local), 'dp'), 'lon')  133 us
    psum x1, blocking collectives, per_device(): lax.psum((point_local, depth_local, bias_local), 'dp')  112 us
    ppermute x10, waiting for transfers between devices, from_behind(): return lax.ppermute(block, axis, route)  61.1 us
    ppermute x10, starting transfers between devices, from_behind(): return lax.ppermute(block, axis, route)  36.7 us
    psum x1, blocking collectives, per_device(): lax.psum(lax.psum((point_local, depth_local, bias_local), 'dp'), 'lon')  16.7 us
  transfers between devices with their start and end apart: 12, of which 4 were waited for; matrix products, arithmetic and copies ran while one was open for 4% of the time, Pallas kernels for 0%

profile of v1, /device:TPU:1, one launch (start us, length us, event | category | flops | bytes accessed | tf_op | source)
XLA Modules:
  0.0 700.2 jit_solution(16211761667689777323)
XLA Ops:
  7.2 5.8 collective-permute-start.8
  13.0 1.4 fusion.71
  14.4 4.8 collective-permute-start
  19.3 2.1 collective-permute-start.1
  21.3 5.4 collective-permute-start.3
  26.8 3.0 collective-permute-start.2
  30.3 42.3 %collective-permute-done.2 = bf16[1,3,48,1152]{3,2,1,0:T(8,128)(2,1)S(1)} collective-permute-done((bf16[1,3,48,1152]{3,2,1,0:T(8,128)(2,1)S(1)}, bf16[1,3,48,1152]{3,2,1,0:T(8,128)(2,1)S(1)}, u32[]{:S(2)}, u32[]{:S(2)}) %collective-permute-start.2) | collective-permute-done | bytes 331808 | tf_op jit(solution)/shard_map/ppermute | solution.py:13
  73.1 1.5 fusion.8
  74.6 1.2 convert_reduce_fusion.1
  76.5 1.2 fusion.67
  77.6 5.8 collective-permute-start.5
  84.4 2.1 collective-permute-start.4
  86.6 3.0 collective-permute-start.6
  89.6 2.0 collective-permute-start.7
  92.3 1.4 fusion.15
  93.7 1.1 convert_reduce_fusion
  95.8 2.3 fusion.41
  98.3 1.5 pad_maximum_fusion
  101.6 18.8 %collective-permute-done.4 = bf16[1,3,48,1152]{3,2,1,0:T(8,128)(2,1)} collective-permute-done((bf16[1,3,48,1152]{3,2,1,0:T(8,128)(2,1)}, bf16[1,3,48,1152]{3,2,1,0:T(8,128)(2,1)}, u32[]{:S(2)}, u32[]{:S(2)}) %collective-permute-start.4) | collective-permute-done | bytes 331808 | tf_op jit(solution)/shard_map/ppermute | solution.py:13
  120.4 1.0 constant_dynamic-update-slice_fusion.5
  121.4 2.7 collective-permute-start.9
  124.8 112.2 %psum.46 = f32[2,256]{1,0:T(2,128)} all-reduce(f32[2,256]{1,0:T(2,128)S(1)} %pad_maximum_fusion.2), channel_id=1, replica_groups=mesh['dp'=64,'lon'=8] {'dp'}, use_global_device_ids=true, to_apply=%region_21.22 | all-reduce | flops 512 | bytes 4096 | tf_op jit(solution)/shard_map/psum | solution.py:146
  236.9 16.7 %psum.47 = f32[2,256]{1,0:T(2,128)S(1)} all-reduce(f32[2,256]{1,0:T(2,128)} %psum.46), channel_id=1, replica_groups=mesh['dp'=64,'lon'=8] {'lon'}, use_global_device_ids=true, to_apply=%region_22.23 | all-reduce | flops 512 | bytes 4096 | tf_op jit(solution)/shard_map/psum | solution.py:145
  255.2 1.2 constant_dynamic-update-slice_fusion.4
  256.3 1.1 fusion.62
  257.6 1.1 constant_dynamic-update-slice_fusion.7
  258.8 290.5 %all-reduce.25.cloned.1.call-done = (f32[2,3,3,1152]{3,2,1,0:T(4,128)}, f32[2,1152,256]{2,1,0:T(8,128)}) async-done(((f32[2,3,3,1152]{3,2,1,0:T(4,128)}, f32[2,1152,256]{2,1,0:T(8,128)}), (f32[2,3,3,1152]{3,2,1,0:T(4,128)}, f32[2,1152,256]{2,1,0:T(8,128)})) %all-reduce.25.cloned.1.call-update) | async-done | bytes 2442256 | tf_op jit(solution)/shard_map/psum | solution.py:146
  549.5 1.2 constant_dynamic-update-slice_fusion.6
  550.7 1.2 fusion.65
  552.1 5.0 fusion.25
  557.1 132.7 %all-reduce.27.cloned.1.call-done = (f32[2,3,3,1152]{3,2,1,0:T(4,128)}, f32[2,1152,256]{2,1,0:T(8,128)}) async-done(((f32[2,3,3,1152]{3,2,1,0:T(4,128)}, f32[2,1152,256]{2,1,0:T(8,128)}), (f32[2,3,3,1152]{3,2,1,0:T(4,128)}, f32[2,1152,256]{2,1,0:T(8,128)})) %all-reduce.27.cloned.1.call-update) | async-done | bytes 2442256 | tf_op jit(solution)/shard_map/psum | solution.py:145
  689.8 2.9 multiply_convert_fusion
  (125 shorter events, 9.3 us)
Async XLA Ops:
  7.2 12.0 %copy-start = (bf16[1,9,48,1152]{3,2,1,0:T(8,128)(2,1)S(1)}, bf16[1,9,48,1152]{3,2,1,0:T(8,128)(2,1)}, u32[]{:S(2)}) copy-start(bf16[1,9,48,1152]{3,2,1,0:T(8,128)(2,1)} %param.5) | copy-start | bytes 2985988
  7.2 542.1 %all-reduce.25.cloned.1.call-start = ((), (), s32[]{:S(2)}) async-start(), calls=%async_computation | async-start | bytes 4939776 | tf_op jit(solution)/shard_map/psum | solution.py:146
  7.2 84.9 %collective-permute-start.8 = (bf16[1,9,48,1152]{3,2,1,0:T(8,128)(2,1)}, bf16[1,9,48,1152]{3,2,1,0:T(8,128)(2,1)S(1)}, u32[]{:S(2)}, u32[]{:S(2)}) collective-permute-start(bf16[1,9,48,1152]{3,2,1,0:T(8,128)(2,1)} %param.5), channel_id=1, source_target_pairs={{4,0},{5,1},{6,2},{7,3},{0,4},{1,5},{2,6},{3,7},{12,8},{13,9},{14,... | collective-permute-start | bytes 2985992 | tf_op jit(solution)/shard_map/ppermute | solution.py:13
  14.4 58.2 %collective-permute-start = (bf16[1,6,48,1152]{3,2,1,0:T(8,128)(2,1)S(1)}, bf16[1,6,48,1152]{3,2,1,0:T(8,128)(2,1)S(1)}, u32[]{:S(2)}, u32[]{:S(2)}) collective-permute-start(bf16[1,6,48,1152]{3,2,1,0:T(8,128)(2,1)S(1)} %get-tuple-element.63), channel_id=1, source_target_pairs={{5,0},{6,1},{7,2},{0,3},{1,4},{2,5},{3,6},{4,7},{13,8},{14,9},{15,... | collective-permute-start | bytes 1990664 | tf_op jit(solution)/shard_map/ppermute | solution.py:13
  19.3 10.7 %copy-start.32 = (f32[2,256]{1,0:T(2,128)S(1)}, f32[2,256]{1,0:T(2,128)}, u32[]{:S(2)}) copy-start(f32[2,256]{1,0:T(2,128)} %param.8) | copy-start | bytes 6148
  19.3 10.7 %copy-start.10 = (bf16[2,3,3,1152]{3,0,2,1:T(2,128)(2,1)S(1)}, bf16[2,3,3,1152]{3,0,2,1:T(2,128)(2,1)}, u32[]{:S(2)}) copy-start(bf16[2,3,3,1152]{3,0,2,1:T(2,128)(2,1)} %param.6) | copy-start | bytes 124420
  19.3 10.9 %copy-start.8 = (bf16[1,9,48,512]{3,2,1,0:T(8,128)(2,1)S(1)}, bf16[1,9,48,512]{3,2,1,0:T(8,128)(2,1)}, u32[]{:S(2)}) copy-start(bf16[1,9,48,512]{3,2,1,0:T(8,128)(2,1)} %param.9) | copy-start | bytes 1327108
  19.3 53.4 %collective-permute-start.1 = (bf16[1,3,48,1152]{3,2,1,0:T(8,128)(2,1)S(1)}, bf16[1,3,48,1152]{3,2,1,0:T(8,128)(2,1)S(1)}, u32[]{:S(2)}, u32[]{:S(2)}) collective-permute-start(bf16[1,3,48,1152]{3,2,1,0:T(8,128)(2,1)S(1)} %get-tuple-element.61), channel_id=1, source_target_pairs={{6,0},{7,1},{0,2},{1,3},{2,4},{3,5},{4,6},{5,7},{14,8},{15,9},{8,1... | collective-permute-start | bytes 995336 | tf_op jit(solution)/shard_map/ppermute | solution.py:13
  21.3 51.5 %collective-permute-start.3 = (bf16[1,6,48,1152]{3,2,1,0:T(8,128)(2,1)S(1)}, bf16[1,6,48,1152]{3,2,1,0:T(8,128)(2,1)S(1)}, u32[]{:S(2)}, u32[]{:S(2)}) collective-permute-start(bf16[1,6,48,1152]{3,2,1,0:T(8,128)(2,1)S(1)} %get-tuple-element.64), channel_id=1, source_target_pairs={{3,0},{4,1},{5,2},{6,3},{7,4},{0,5},{1,6},{2,7},{11,8},{12,9},{13,... | collective-permute-start | bytes 1990664 | tf_op jit(solution)/shard_map/ppermute | solution.py:13
  26.8 45.8 %collective-permute-start.2 = (bf16[1,3,48,1152]{3,2,1,0:T(8,128)(2,1)S(1)}, bf16[1,3,48,1152]{3,2,1,0:T(8,128)(2,1)S(1)}, u32[]{:S(2)}, u32[]{:S(2)}) collective-permute-start(bf16[1,3,48,1152]{3,2,1,0:T(8,128)(2,1)S(1)} %get-tuple-element.62), channel_id=1, source_target_pairs={{2,0},{3,1},{4,2},{5,3},{6,4},{7,5},{0,6},{1,7},{10,8},{11,9},{12,... | collective-permute-start | bytes 995336 | tf_op jit(solution)/shard_map/ppermute | solution.py:13
  30.2 42.8 %copy-start.14 = (f32[1152]{0:T(1024)}, f32[1152]{0:T(1024)S(1)}, u32[]{:S(2)}) copy-start(f32[1152]{0:T(1024)S(1)} %get-tuple-element.23) | copy-start | bytes 13828
  30.2 42.8 %copy-start.16 = (f32[1152]{0:T(1024)}, f32[1152]{0:T(1024)S(1)}, u32[]{:S(2)}) copy-start(f32[1152]{0:T(1024)S(1)} %get-tuple-element.31) | copy-start | bytes 13828
  30.2 42.8 %copy-start.18 = (f32[1152]{0:T(1024)}, f32[1152]{0:T(1024)S(1)}, u32[]{:S(2)}) copy-start(f32[1152]{0:T(1024)S(1)} %get-tuple-element.32) | copy-start | bytes 13828
  30.2 42.8 %copy-start.20 = (f32[1152]{0:T(1024)}, f32[1152]{0:T(1024)S(1)}, u32[]{:S(2)}) copy-start(f32[1152]{0:T(1024)S(1)} %get-tuple-element.33) | copy-start | bytes 13828
  30.2 42.8 %copy-start.22 = (f32[1152]{0:T(1024)}, f32[1152]{0:T(1024)S(1)}, u32[]{:S(2)}) copy-start(f32[1152]{0:T(1024)S(1)} %get-tuple-element.34) | copy-start | bytes 13828
  30.3 42.8 %copy-start.24 = (f32[1152]{0:T(1024)}, f32[1152]{0:T(1024)S(1)}, u32[]{:S(2)}) copy-start(f32[1152]{0:T(1024)S(1)} %get-tuple-element.35) | copy-start | bytes 13828
  30.3 42.8 %copy-start.26 = (f32[1152]{0:T(1024)}, f32[1152]{0:T(1024)S(1)}, u32[]{:S(2)}) copy-start(f32[1152]{0:T(1024)S(1)} %get-tuple-element.36) | copy-start | bytes 13828
  30.3 42.8 %copy-start.28 = (f32[1152]{0:T(1024)}, f32[1152]{0:T(1024)S(1)}, u32[]{:S(2)}) copy-start(f32[1152]{0:T(1024)S(1)} %get-tuple-element.37) | copy-start | bytes 13828
  30.3 42.8 %copy-start.30 = (f32[1152]{0:T(1024)}, f32[1152]{0:T(1024)S(1)}, u32[]{:S(2)}) copy-start(f32[1152]{0:T(1024)S(1)} %get-tuple-element.38) | copy-start | bytes 13828
  30.3 62.0 %copy-start.12 = (f32[1152]{0:T(1024)}, f32[1152]{0:T(1024)S(1)}, u32[]{:S(2)}) copy-start(f32[1152]{0:T(1024)S(1)} %get-tuple-element.40) | copy-start | bytes 13828
  77.6 177.5 %collective-permute-start.5 = (bf16[1,6,48,1152]{3,2,1,0:T(8,128)(2,1)}, bf16[1,6,48,1152]{3,2,1,0:T(8,128)(2,1)}, u32[]{:S(2)}, u32[]{:S(2)}) collective-permute-start(bf16[1,6,48,1152]{3,2,1,0:T(8,128)(2,1)} %get-tuple-element.55), channel_id=1, source_target_pairs={{3,0},{4,1},{5,2},{6,3},{7,4},{0,5},{1,6},{2,7},{11,8},{12,9},{13,... | collective-permute-start | bytes 1990664 | tf_op jit(solution)/shard_map/ppermute | solution.py:13
  84.4 36.0 %collective-permute-start.4 = (bf16[1,3,48,1152]{3,2,1,0:T(8,128)(2,1)}, bf16[1,3,48,1152]{3,2,1,0:T(8,128)(2,1)}, u32[]{:S(2)}, u32[]{:S(2)}) collective-permute-start(bf16[1,3,48,1152]{3,2,1,0:T(8,128)(2,1)} %get-tuple-element.57), channel_id=1, source_target_pairs={{2,0},{3,1},{4,2},{5,3},{6,4},{7,5},{0,6},{1,7},{10,8},{11,9},{12,... | collective-permute-start | bytes 995336 | tf_op jit(solution)/shard_map/ppermute | solution.py:13
  86.6 171.1 %collective-permute-start.6 = (bf16[1,6,48,1152]{3,2,1,0:T(8,128)(2,1)}, bf16[1,6,48,1152]{3,2,1,0:T(8,128)(2,1)}, u32[]{:S(2)}, u32[]{:S(2)}) collective-permute-start(bf16[1,6,48,1152]{3,2,1,0:T(8,128)(2,1)} %get-tuple-element.56), channel_id=1, source_target_pairs={{5,0},{6,1},{7,2},{0,3},{1,4},{2,5},{3,6},{4,7},{13,8},{14,9},{15,... | collective-permute-start | bytes 1990664 | tf_op jit(solution)/shard_map/ppermute | solution.py:13
  89.6 459.9 %collective-permute-start.7 = (bf16[1,3,48,1152]{3,2,1,0:T(8,128)(2,1)}, bf16[1,3,48,1152]{3,2,1,0:T(8,128)(2,1)}, u32[]{:S(2)}, u32[]{:S(2)}) collective-permute-start(bf16[1,3,48,1152]{3,2,1,0:T(8,128)(2,1)} %get-tuple-element.58), channel_id=1, source_target_pairs={{6,0},{7,1},{0,2},{1,3},{2,4},{3,5},{4,6},{5,7},{14,8},{15,9},{8,1... | collective-permute-start | bytes 995336 | tf_op jit(solution)/shard_map/ppermute | solution.py:13
  100.7 589.1 %all-reduce.27.cloned.1.call-start = ((), (), s32[]{:S(2)}) async-start(), calls=%async_computation.1 | async-start | bytes 4939776 | tf_op jit(solution)/shard_map/psum | solution.py:145
  121.4 429.3 %collective-permute-start.9 = (bf16[1,9,48,1152]{3,2,1,0:T(8,128)(2,1)S(1)}, bf16[1,9,48,1152]{3,2,1,0:T(8,128)(2,1)}, u32[]{:S(2)}, u32[]{:S(2)}) collective-permute-start(bf16[1,9,48,1152]{3,2,1,0:T(8,128)(2,1)S(1)} %bitcast.70), channel_id=1, source_target_pairs={{4,0},{5,1},{6,2},{7,3},{0,4},{1,5},{2,6},{3,7},{12,8},{13,9},{14,... | collective-permute-start | bytes 2985992 | tf_op jit(solution)/shard_map/ppermute | solution.py:13
  549.3 2.6 copy-start.2
  549.3 2.6 copy-start.3
  549.3 2.6 copy-start.4
  549.3 2.6 copy-start.5
  549.3 2.6 copy-start.6
  689.7 2.9 copy-start.11
  (13 other events, 31.3 us)
Sparse Core Ops, SparseCore 0:
  100.8 448.4 all-reduce.24
  552.6 137.0 all-reduce.26
